TPU v7x, 32 devices: a whole 2x2x4 slice. The times are simulated.
32 devices in a mesh: groups: 2 (over x), tok: 16 (over z, y, core).
Axes of the slice: x: 2, y: 2, z: 4, core: 2. Of those that a mesh axis runs over, the one named last changes fastest.
Arguments:
- latents: bfloat16 [2304, 1536], P(('groups', 'tok')), parts along dimension 0, may hold values from -6 to 6
- fresh_noise: bfloat16 [2304, 1536], P(('groups', 'tok')), parts along dimension 0, may hold values from -6 to 6
- levels: int32 [4], replicated, may hold values from 50 to 996, as said below
- time_weight: bfloat16 [256, 3072], replicated, may hold values from -0.375 to 0.375
- w_query: bfloat16 [1536, 768], replicated, may hold values from -1 to 1
- w_key: bfloat16 [1536, 768], replicated, may hold values from -10 to 10
- w_value: bfloat16 [1536, 768], replicated, may hold values from -0.15625 to 0.15625
- w_out: bfloat16 [768, 1536], replicated, may hold values from -0.21875 to 0.21875
Outputs:
- stepped: bfloat16 [2, 2304, 1536], P(None, ('groups', 'tok')), parts along dimension 1
- velocity: bfloat16 [2, 2304, 1536], P(None, ('groups', 'tok')), parts along dimension 1
There are 2 independent parts, one for each index of `groups`. A program takes and returns all parts, laid end to end along the dimension named above; an argument that names none is the same for every part. Nothing has to cross between parts.
Inputs may be any that keep to these rules, and one draw needn't show every extreme that they name: `levels`: strictly increasing over sections.
All inputs are finite; a program needn't handle non-finite values.
Results may differ from a plain program's by a relative error of at most 0.0095.
Values may be sent and summed in bfloat16 or wider, within the bound.
No kernel may reach another device: no remote copies, remote signals or barrier semaphores. Data moves between devices by JAX's collectives and lax.ppermute only.
A program may use at most 128 MiB of HBM per device.

v0:
```python
import math
import jax
import jax.numpy as jnp
from jax import lax
from jax.sharding import PartitionSpec as P

D = 1536
HEADS = 6
HEAD_DIM = 128
TFREQ = 256
SECTIONS = 4
epsilon = 1e-06


def shifted(block, axis, distance):
    devices = range(lax.axis_size(axis))
    route = [(i - distance, i) for i in devices if i - distance in devices]
    return lax.ppermute(block, axis, route)


def embed_level(level_value, time_weight):
    half_width = TFREQ // 2
    frequency = jnp.exp(-math.log(10000.0) * jnp.arange(half_width, dtype=jnp.float32) / half_width)
    angles = level_value.astype(jnp.float32) * frequency
    embedding = jnp.concatenate([jnp.cos(angles), jnp.sin(angles)])[None, :]
    modulated = jnp.dot(
        embedding, time_weight.astype(jnp.float32), precision=lax.Precision.HIGHEST
    )[0]
    return (modulated[:D], modulated[D:])


def body(latents, fresh_noise, levels, time_weight, w_query, w_key, w_value, w_out):
    local_rows = latents.shape[0]
    per_section = lax.axis_size("tok") // SECTIONS
    span_rows = local_rows * per_section
    my_block = lax.axis_index("tok") // per_section
    section_ids = jnp.arange(SECTIONS, dtype=jnp.int32)
    my_level = jnp.sum(jnp.where(section_ids == my_block, levels, 0))
    prev_level = jnp.sum(jnp.where(section_ids == my_block - 1, levels, 0))
    step_size = (prev_level - my_level).astype(jnp.float32) / 1000.0
    shift_vec, scale_vec = embed_level(my_level, time_weight)

    def denoise_local(rows):
        rows_f = rows.astype(jnp.float32)
        normed = rows_f * lax.rsqrt(jnp.mean(rows_f * rows_f, axis=-1, keepdims=True) + epsilon)
        hidden = (normed * (1.0 + scale_vec) + shift_vec).astype(jnp.bfloat16)
        queries = jnp.dot(hidden, w_query, preferred_element_type=jnp.float32).astype(jnp.bfloat16)
        queries = queries.reshape(local_rows, HEADS, HEAD_DIM)
        local_keys = jnp.dot(hidden, w_key, preferred_element_type=jnp.float32).astype(jnp.bfloat16)
        local_values = jnp.dot(hidden, w_value, preferred_element_type=jnp.float32).astype(
            jnp.bfloat16
        )
        gathered_keys, gathered_values = (
            lax.all_gather(local_keys, "tok", axis=0, tiled=True),
            lax.all_gather(local_values, "tok", axis=0, tiled=True),
        )
        best = jnp.full((HEADS, local_rows), -1e30, jnp.float32)
        count = gathered_keys.shape[0]
        key_blocks = jnp.arange(count, dtype=jnp.int32) // span_rows
        allowed = (key_blocks <= my_block)[None, None, :]
        scores = jnp.einsum(
            "rhd,phd->hrp",
            queries,
            gathered_keys.reshape(count, HEADS, HEAD_DIM),
            preferred_element_type=jnp.float32,
        ) / math.sqrt(HEAD_DIM)
        scores = jnp.where(allowed, scores, -1e30)
        new_best = jnp.maximum(best, jnp.max(scores, axis=-1))
        weights = jnp.where(allowed, jnp.exp(scores - new_best[..., None]), 0.0)
        denominator = jnp.sum(weights, axis=-1)
        summed = jnp.einsum(
            "hrp,phd->hrd",
            weights.astype(jnp.bfloat16),
            gathered_values.reshape(count, HEADS, HEAD_DIM),
            preferred_element_type=jnp.float32,
        )
        result = (new_best, denominator, summed)
        best, denominator, summed = result
        attended = (summed / denominator[..., None]).astype(jnp.bfloat16)
        attended = attended.transpose(1, 0, 2).reshape(local_rows, HEADS * HEAD_DIM)
        moving = jnp.dot(attended, w_out, preferred_element_type=jnp.float32)
        stepped = (rows_f + step_size * moving).astype(jnp.bfloat16)
        return (stepped, moving.astype(jnp.bfloat16))

    first, first_moving = denoise_local(latents)
    incoming = shifted(first, "tok", -per_section)
    second_input = jnp.where(my_block == SECTIONS - 1, fresh_noise, incoming)
    second, second_moving = denoise_local(second_input)
    return (jnp.stack([first, second]), jnp.stack([first_moving, second_moving]))


def solution(mesh):
    return jax.shard_map(
        body,
        mesh=mesh,
        in_specs=(
            P(("groups", "tok"), None),
            P(("groups", "tok"), None),
            P(),
            P(),
            P(),
            P(),
            P(),
            P(),
        ),
        out_specs=(P(None, ("groups", "tok"), None), P(None, ("groups", "tok"), None)),
        check_vma=False,
    )
```

profile of v0, /device:TPU:0, one launch (start us, length us, event | category | flops | bytes accessed | tf_op | source)
XLA Modules:
  0.0 216.5 jit_solution(2579585131314085424)
XLA Ops:
  7.2 0.0 copy-start
  7.2 0.0 copy-start.3
  7.2 0.0 all-gather.5.cloned.1.call-start
  7.3 1.5 fusion.47
  9.4 2.1 fusion.65
  11.5 1.1 fusion.22
  12.6 0.0 copy-done.3
  12.6 2.9 %convolution_convert_fusion.4 = bf16[72,768]{1,0:T(8,128)(2,1)} fusion(bf16[1536,768]{1,0:T(8,128)(2,1)} %param.13, bf16[72,1536]{1,0:T(8,128)(2,1)S(1)} %copy-done.3, f32[1536]{0:T(1024)S(1)} %get-tuple-element.11, f32[1536]{0:T(1024)S(1)} %get-tuple-element.10, f32[72]{0:T(128)S(1)} %add_rsqrt_fusion.1), kind=kOutput, calls=%fused_computation.20 | convolution fusion | flops 170477568 | bytes 2703648 | tf_op jit(solution)/shard_map/dot_general | solution.py:49
  15.5 0.0 all-gather.5.cloned.1.call-update
  15.6 0.0 all-gather.7.cloned.1.call-start
  15.6 2.9 %convolution_convert_fusion.3 = bf16[72,768]{1,0:T(8,128)(2,1)} fusion(bf16[1536,768]{1,0:T(8,128)(2,1)} %param.14, bf16[72,1536]{1,0:T(8,128)(2,1)S(1)} %copy-done.3, f32[1536]{0:T(1024)S(1)} %get-tuple-element.11, f32[1536]{0:T(1024)S(1)} %get-tuple-element.10, f32[72]{0:T(128)S(1)} %add_rsqrt_fusion.1), kind=kOutput, calls=%fused_computation.19 | convolution fusion | flops 170477568 | bytes 2703648 | tf_op jit(solution)/shard_map/dot_general | solution.py:50
  18.5 0.0 all-gather.7.cloned.1.call-update
  18.5 0.0 all-gather.9.cloned.1.call-start
  19.7 2.2 %fusion.12 = bf16[9,6,8,128]{3,2,1,0:T(8,128)(2,1)S(1)} fusion(bf16[1536,768]{1,0:T(8,128)(2,1)} %param.12, bf16[72,1536]{1,0:T(8,128)(2,1)S(1)} %copy-done.3, f32[1536]{0:T(1024)S(1)} %get-tuple-element.11, f32[1536]{0:T(1024)S(1)} %get-tuple-element.10, f32[72]{0:T(128)S(1)} %add_rsqrt_fusion.1), kind=kOutput, calls=%fused_computation.24 | convolution fusion | flops 170477568 | bytes 2703648 | tf_op jit(solution)/shard_map/dot_general | solution.py:47
  22.0 36.7 %all-gather.5.cloned.1.call-done = bf16[1152,768]{1,0:T(8,128)(2,1)} async-done(((bf16[72,768]{1,0:T(8,128)(2,1)}), bf16[1152,768]{1,0:T(8,128)(2,1)}) %all-gather.5.cloned.1.call-update) | async-done | bytes 1769488 | tf_op jit(solution)/shard_map/all_gather | solution.py:54
  58.7 3.9 %copy.16 = bf16[1152,768]{0,1:T(8,128)(2,1)} copy(bf16[1152,768]{1,0:T(8,128)(2,1)} %all-gather.5.cloned.1.call-done) | data formatting | bytes 3538944 | tf_op jit(solution)/shard_map/all_gather | solution.py:54
  62.6 2.1 fusion.59
  64.6 0.0 copy-start.2
  64.6 1.3 copy-done.2
  65.9 0.5 fusion.2
  66.4 34.1 %all-gather.7.cloned.1.call-done = bf16[1152,768]{1,0:T(8,128)(2,1)} async-done(((bf16[72,768]{1,0:T(8,128)(2,1)}), bf16[1152,768]{1,0:T(8,128)(2,1)}) %all-gather.7.cloned.1.call-update) | async-done | bytes 1769488 | tf_op jit(solution)/shard_map/all_gather | solution.py:55
  100.5 3.9 %copy.19 = bf16[1152,768]{0,1:T(8,128)(2,1)} copy(bf16[1152,768]{1,0:T(8,128)(2,1)} %all-gather.7.cloned.1.call-done) | data formatting | bytes 3538944 | tf_op jit(solution)/shard_map/all_gather | solution.py:55
  104.4 3.0 %fusion.11 = bf16[6,9,8,128]{3,2,1,0:T(8,128)(2,1)S(1)} fusion(bf16[1152,6,128]{0,2,1:T(8,128)(2,1)} %bitcast.76, f32[6,72,1152]{2,1,0:T(8,128)} %copy-done.2, f32[6,72]{1,0:T(8,128)S(1)} %broadcast_maximum_fusion.1, pred[1152]{0:T(1024)(128)(4,1)S(1)} %fusion.43, f32[72,6]{0,1:T(8,128)S(1)} %bitcast.80), kind=kOutput, calls=%fused_computation.23 | convolution fusion | flops 129005568 | bytes 3875328 | tf_op jit(solution)/shard_map/hrp,phd->hrd/dot_general | solution.py:71
  107.4 0.0 copy-done
  107.4 0.0 copy-start.4
  107.4 0.5 convert_bitcast_fusion.1
  108.0 1.3 collective-permute-start
  109.3 8.3 %collective-permute-done = bf16[72,1536]{1,0:T(8,128)(2,1)} collective-permute-done((bf16[72,1536]{1,0:T(8,128)(2,1)S(1)}, bf16[72,1536]{1,0:T(8,128)(2,1)}, u32[]{:S(2)}, u32[]{:S(2)}) %collective-permute-start) | collective-permute-done | bytes 221216 | tf_op jit(solution)/shard_map/ppermute | solution.py:18
  117.5 0.0 copy-done.4
  117.5 1.1 fusion.27
  118.7 2.9 %convolution_convert_fusion.1 = bf16[72,768]{1,0:T(8,128)(2,1)} fusion(bf16[1536,768]{1,0:T(8,128)(2,1)} %param.13, bf16[72,1536]{1,0:T(8,128)(2,1)S(1)} %get-tuple-element.5, f32[72]{0:T(128)S(1)} %add_rsqrt_fusion, f32[1536]{0:T(1024)S(1)} %get-tuple-element.11, f32[1536]{0:T(1024)S(1)} %get-tuple-element.10), kind=kOutput, calls=%fused_computation.17 | convolution fusion | flops 170477568 | bytes 2703648 | tf_op jit(solution)/shard_map/dot_general | solution.py:49
  121.6 0.0 all-gather.9.cloned.1.call-update
  121.6 0.0 all-gather.11.cloned.1.call-start
  121.6 2.9 %convolution_convert_fusion = bf16[72,768]{1,0:T(8,128)(2,1)} fusion(bf16[1536,768]{1,0:T(8,128)(2,1)} %param.14, bf16[72,1536]{1,0:T(8,128)(2,1)S(1)} %get-tuple-element.5, f32[72]{0:T(128)S(1)} %add_rsqrt_fusion, f32[1536]{0:T(1024)S(1)} %get-tuple-element.11, f32[1536]{0:T(1024)S(1)} %get-tuple-element.10), kind=kOutput, calls=%fused_computation.16 | convolution fusion | flops 170477568 | bytes 2703648 | tf_op jit(solution)/shard_map/dot_general | solution.py:50
  124.5 0.0 all-gather.11.cloned.1.call-update
  124.6 2.3 %fusion.13 = bf16[9,6,8,128]{3,2,1,0:T(8,128)(2,1)S(1)} fusion(bf16[1536,768]{1,0:T(8,128)(2,1)} %param.12, bf16[72,1536]{1,0:T(8,128)(2,1)S(1)} %get-tuple-element.5, f32[72]{0:T(128)S(1)} %add_rsqrt_fusion, f32[1536]{0:T(1024)S(1)} %get-tuple-element.11, f32[1536]{0:T(1024)S(1)} %get-tuple-element.10), kind=kOutput, calls=%fused_computation.25 | convolution fusion | flops 170477568 | bytes 2703648 | tf_op jit(solution)/shard_map/dot_general | solution.py:47
  126.8 32.5 %all-gather.9.cloned.1.call-done = bf16[1152,768]{1,0:T(8,128)(2,1)} async-done(((bf16[72,768]{1,0:T(8,128)(2,1)}), bf16[1152,768]{1,0:T(8,128)(2,1)}) %all-gather.9.cloned.1.call-update) | async-done | bytes 1769488 | tf_op jit(solution)/shard_map/all_gather | solution.py:54
  159.3 3.9 %copy.22 = bf16[1152,768]{0,1:T(8,128)(2,1)} copy(bf16[1152,768]{1,0:T(8,128)(2,1)} %all-gather.9.cloned.1.call-done) | data formatting | bytes 3538944 | tf_op jit(solution)/shard_map/all_gather | solution.py:54
  163.1 2.1 fusion.60
  165.2 0.0 copy-start.1
  165.2 1.3 copy-done.1
  166.5 0.5 fusion.4
  167.0 34.0 %all-gather.11.cloned.1.call-done = bf16[1152,768]{1,0:T(8,128)(2,1)} async-done(((bf16[72,768]{1,0:T(8,128)(2,1)}), bf16[1152,768]{1,0:T(8,128)(2,1)}) %all-gather.11.cloned.1.call-update) | async-done | bytes 1769488 | tf_op jit(solution)/shard_map/all_gather | solution.py:55
  201.0 3.9 %copy.25 = bf16[1152,768]{0,1:T(8,128)(2,1)} copy(bf16[1152,768]{1,0:T(8,128)(2,1)} %all-gather.11.cloned.1.call-done) | data formatting | bytes 3538944 | tf_op jit(solution)/shard_map/all_gather | solution.py:55
  204.8 3.0 %fusion.10 = bf16[6,9,8,128]{3,2,1,0:T(8,128)(2,1)S(1)} fusion(bf16[1152,6,128]{0,2,1:T(8,128)(2,1)} %bitcast.75, f32[6,72,1152]{2,1,0:T(8,128)} %copy-done.1, f32[6,72]{1,0:T(8,128)S(1)} %broadcast_maximum_fusion, pred[1152]{0:T(1024)(128)(4,1)S(1)} %fusion.43, f32[72,6]{0,1:T(8,128)S(1)} %bitcast.79), kind=kOutput, calls=%fused_computation.22 | convolution fusion | flops 129005568 | bytes 3875328 | tf_op jit(solution)/shard_map/hrp,phd->hrd/dot_general | solution.py:71
  207.8 0.5 convert_bitcast_fusion
  208.4 0.8 pad_maximum_fusion.1
  209.2 0.8 pad_maximum_fusion
  (8 shorter events, 0.1 us)
Async XLA Ops:
  7.2 100.2 %copy-start = (bf16[768,1536]{1,0:T(8,128)(2,1)S(1)}, bf16[768,1536]{1,0:T(8,128)(2,1)}, u32[]{:S(2)}) copy-start(bf16[768,1536]{1,0:T(8,128)(2,1)} %param.15) | copy-start | bytes 7077892
  7.2 5.5 %copy-start.3 = (bf16[72,1536]{1,0:T(8,128)(2,1)S(1)}, bf16[72,1536]{1,0:T(8,128)(2,1)}, u32[]{:S(2)}) copy-start(bf16[72,1536]{1,0:T(8,128)(2,1)} %param.8) | copy-start | bytes 663556
  7.2 51.5 %all-gather.5.cloned.1.call-start = ((), (), s32[]{:S(2)}) async-start(), calls=%async_computation | async-start | bytes 1880064 | tf_op jit(solution)/shard_map/all_gather | solution.py:54
  15.6 85.0 %all-gather.7.cloned.1.call-start = ((), (), s32[]{:S(2)}) async-start(), calls=%async_computation.1 | async-start | bytes 1880064 | tf_op jit(solution)/shard_map/all_gather | solution.py:55
  18.5 140.8 %all-gather.9.cloned.1.call-start = ((), (), s32[]{:S(2)}) async-start(), calls=%async_computation.2 | async-start | bytes 1880064 | tf_op jit(solution)/shard_map/all_gather | solution.py:54
  64.6 1.3 copy-start.2
  107.4 10.1 %copy-start.4 = (bf16[72,1536]{1,0:T(8,128)(2,1)S(1)}, bf16[72,1536]{1,0:T(8,128)(2,1)}, u32[]{:S(2)}) copy-start(bf16[72,1536]{1,0:T(8,128)(2,1)} %param.9) | copy-start | bytes 663556
  108.0 9.6 %collective-permute-start = (bf16[72,1536]{1,0:T(8,128)(2,1)S(1)}, bf16[72,1536]{1,0:T(8,128)(2,1)}, u32[]{:S(2)}, u32[]{:S(2)}) collective-permute-start(bf16[72,1536]{1,0:T(8,128)(2,1)S(1)} %get-tuple-element.7), channel_id=1, source_target_pairs={{4,0},{5,1},{6,2},{7,3},{8,4},{9,5},{10,6},{11,7},{12,8},{13,9},{1... | collective-permute-start | bytes 663560 | tf_op jit(solution)/shard_map/ppermute | solution.py:18
  121.6 79.4 %all-gather.11.cloned.1.call-start = ((), (), s32[]{:S(2)}) async-start(), calls=%async_computation.3 | async-start | bytes 1880064 | tf_op jit(solution)/shard_map/all_gather | solution.py:55
  165.2 1.3 copy-start.1
Sparse Core Ops, SparseCore 0:
  15.7 42.9 all-gather.4
  61.4 39.0 all-gather.6
  121.7 37.5 all-gather.8
  161.9 39.0 all-gather.10
where the time goes:
time: 217 us
  waiting for transfers between devices  146 us (67%)
  matrix products  29.4 us (14%)
  local copies, waits for them, and re-layouts  18 us (8%)
  between operations  15.6 us (7%)
  other arithmetic  6.41 us (3%)
    all_gather x2, waiting for transfers between devices, denoise_local(): lax.all_gather(local_keys, 'tok', axis=0, tiled=True)  69.2 us
    all_gather x2, waiting for transfers between devices, denoise_local(): lax.all_gather(local_values, 'tok', axis=0, tiled=True)  68.1 us
    ppermute x1, waiting for transfers between devices, shifted(): return lax.ppermute(block, axis, route)  8.25 us
    all_gather x2, local copies, waits for them, and re-layouts, denoise_local(): lax.all_gather(local_keys, 'tok', axis=0, tiled=True)  7.7 us
    all_gather x2, local copies, waits for them, and re-layouts, denoise_local(): lax.all_gather(local_values, 'tok', axis=0, tiled=True)  7.7 us
    dot_general x2, matrix products, denoise_local(): jnp.einsum('hrp,phd->hrd', weights.astype(jnp.bfloat16), gathered_values....  5.99 us
    dot_general x2, matrix products, denoise_local(): jnp.dot(hidden, w_key, preferred_element_type=jnp.float32)  5.8 us
    dot_general x2, matrix products, denoise_local(): jnp.dot(hidden, w_value, preferred_element_type=jnp.float32)  5.79 us
  transfers between devices with their start and end apart: 5, of which 5 were waited for; matrix products, arithmetic and copies ran while one was open for 11% of the time, Pallas kernels for 0%

commit v1 on v0

--- a/solution.py
+++ b/solution.py
@@ -10,6 +10,27 @@
 TFREQ = 256
 SECTIONS = 4
 epsilon = 1e-06
+
+
+def ring_gather(value, axis, dim):
+    peers, place, rows = (lax.axis_size(axis), lax.axis_index(axis), value.shape[dim])
+    upward = [(i, (i + 1) % peers) for i in range(peers)]
+    left = [(i, (i - 1) % peers) for i in range(peers)]
+    out = jnp.zeros((*value.shape[:dim], peers * rows, *value.shape[dim + 1 :]), value.dtype)
+    out = lax.dynamic_update_slice_in_dim(out, value, place * rows, axis=dim)
+    from_left = from_right = value
+    half = peers // 2
+    for step in range(1, half + 1):
+        from_left = lax.ppermute(from_left, axis, upward)
+        out = lax.dynamic_update_slice_in_dim(
+            out, from_left, (place - step) % peers * rows, axis=dim
+        )
+        if step < peers - half:
+            from_right = lax.ppermute(from_right, axis, left)
+            out = lax.dynamic_update_slice_in_dim(
+                out, from_right, (place + step) % peers * rows, axis=dim
+            )
+    return out
 
 
 def shifted(block, axis, distance):
@@ -51,7 +72,7 @@
             jnp.bfloat16
         )
         gathered_keys, gathered_values = (
-            lax.all_gather(local_keys, "tok", axis=0, tiled=True),
+            ring_gather(local_keys, "tok", 0),
             lax.all_gather(local_values, "tok", axis=0, tiled=True),
         )
         best = jnp.full((HEADS, local_rows), -1e30, jnp.float32)

time: 217 us -> 313 us (1.44); the launches traced: 217 us -> 308 us
  local copies, waits for them, and re-layouts: 18 us -> 152 us
  waiting for transfers between devices: 146 us -> 42.9 us
  starting transfers between devices: 1.45 us -> 65.5 us
  matrix products: 29.4 us -> 25.6 us
    dynamic_update_slice x0 -> x32, local copies, waits for them, and re-layouts: none -> 118 us  [the longest x16 58.8 us: ring_gather(): lax.dynamic_update_slice_in_dim(out, from_left, (place - step) % peers *...]
    all_gather x2 -> x0, waiting for transfers between devices: 69.2 us -> none  [denoise_local(): lax.all_gather(local_keys, 'tok', axis=0, tiled=True)]
    all_gather x2, waiting for transfers between devices: 68.1 us -> 0.04 us  [denoise_local(): lax.all_gather(local_values, 'tok', axis=0, tiled=True)]
    ppermute x0 -> x30, starting transfers between devices: none -> 64.2 us  [the longest x14 63.2 us: ring_gather(): from_right = lax.ppermute(from_right, axis, left)]
    ppermute x0 -> x30, waiting for transfers between devices: none -> 36.3 us  [the longest x16 34.4 us: ring_gather(): from_left = lax.ppermute(from_left, axis, upward)]
    ppermute x0 -> x30, local copies, waits for them, and re-layouts: none -> 20.1 us  [the longest x16 11.6 us: ring_gather(): from_left = lax.ppermute(from_left, axis, upward)]
    all_gather x2 -> x0, local copies, waits for them, and re-layouts: 7.7 us -> none  [denoise_local(): lax.all_gather(local_keys, 'tok', axis=0, tiled=True)]
  transfers between devices with their start and end apart: 5 -> 33, of which waited for: 5 -> 15; matrix products, arithmetic and copies ran while one was open for 11% -> 50% of each run, Pallas kernels for 0% -> 0%
where the time goes in v1:
time: 313 us; the launch traced here: 308 us
  local copies, waits for them, and re-layouts  152 us (49%)
  starting transfers between devices  65.5 us (21%)
  waiting for transfers between devices  42.9 us (14%)
  matrix products  25.6 us (8%)
  between operations  16.9 us (5%)
  other arithmetic  5.52 us (2%)
    ppermute x14, starting transfers between devices, ring_gather(): from_right = lax.ppermute(from_right, axis, left)  63.2 us
    dynamic_update_slice x16, local copies, waits for them, and re-layouts, ring_gather(): lax.dynamic_update_slice_in_dim(out, from_left, (place - step) % peers *...  58.8 us
    dynamic_update_slice x14, local copies, waits for them, and re-layouts, ring_gather(): lax.dynamic_update_slice_in_dim(out, from_right, (place + step) % peers *...  52.5 us
    ppermute x16, waiting for transfers between devices, ring_gather(): from_left = lax.ppermute(from_left, axis, upward)  34.4 us
    ppermute x16, local copies, waits for them, and re-layouts, ring_gather(): from_left = lax.ppermute(from_left, axis, upward)  11.6 us
    ppermute x14, local copies, waits for them, and re-layouts, ring_gather(): from_right = lax.ppermute(from_right, axis, left)  8.55 us
    all_gather x2, local copies, waits for them, and re-layouts, denoise_local(): lax.all_gather(local_values, 'tok', axis=0, tiled=True)  7.72 us
    dynamic_update_slice x2, local copies, waits for them, and re-layouts, ring_gather(): out = lax.dynamic_update_slice_in_dim(out, value, place * rows, axis=dim)  6.69 us
  transfers between devices with their start and end apart: 33, of which 15 were waited for; matrix products, arithmetic and copies ran while one was open for 50% of the time, Pallas kernels for 0%

profile of v1, /device:TPU:0, one launch (start us, length us, event | category | flops | bytes accessed | tf_op | source)
XLA Modules:
  0.0 308.2 jit_solution(14825002290798596016)
XLA Ops:
  18.7 5.0 %collective-permute-start.1 = (bf16[72,768]{1,0:T(8,128)(2,1)S(1)}, bf16[72,768]{1,0:T(8,128)(2,1)S(1)}, u32[]{:S(2)}, u32[]{:S(2)}) collective-permute-start(bf16[72,768]{1,0:T(8,128)(2,1)S(1)} %convolution_convert_fusion.4), channel_id=1, source_target_pairs={{0,15},{1,0},{2,1},{3,2},{4,3},{5,4},{6,5},{7,6},{8,7},{9,8},{10,9... | collective-permute-start | bytes 331784 | tf_op jit(solution)/shard_map/ppermute | solution.py:29
  26.2 4.4 %collective-permute-start.3 = (bf16[72,768]{1,0:T(8,128)(2,1)S(1)}, bf16[72,768]{1,0:T(8,128)(2,1)S(1)}, u32[]{:S(2)}, u32[]{:S(2)}) collective-permute-start(bf16[72,768]{1,0:T(8,128)(2,1)S(1)} %collective-permute-done.1), channel_id=1, source_target_pairs={{0,15},{1,0},{2,1},{3,2},{4,3},{5,4},{6,5},{7,6},{8,7},{9,8},{10,9... | collective-permute-start | bytes 331784 | tf_op jit(solution)/shard_map/ppermute | solution.py:29
  30.6 3.9 %collective-permute-done.2 = bf16[72,768]{1,0:T(8,128)(2,1)S(1)} collective-permute-done((bf16[72,768]{1,0:T(8,128)(2,1)S(1)}, bf16[72,768]{1,0:T(8,128)(2,1)S(1)}, u32[]{:S(2)}, u32[]{:S(2)}) %collective-permute-start.2) | collective-permute-done | bytes 110624 | tf_op jit(solution)/shard_map/ppermute | solution.py:24
  34.5 4.4 %collective-permute-start.5 = (bf16[72,768]{1,0:T(8,128)(2,1)S(1)}, bf16[72,768]{1,0:T(8,128)(2,1)S(1)}, u32[]{:S(2)}, u32[]{:S(2)}) collective-permute-start(bf16[72,768]{1,0:T(8,128)(2,1)S(1)} %collective-permute-done.3), channel_id=1, source_target_pairs={{0,15},{1,0},{2,1},{3,2},{4,3},{5,4},{6,5},{7,6},{8,7},{9,8},{10,9... | collective-permute-start | bytes 331784 | tf_op jit(solution)/shard_map/ppermute | solution.py:29
  41.5 4.4 %collective-permute-start.7 = (bf16[72,768]{1,0:T(8,128)(2,1)S(1)}, bf16[72,768]{1,0:T(8,128)(2,1)S(1)}, u32[]{:S(2)}, u32[]{:S(2)}) collective-permute-start(bf16[72,768]{1,0:T(8,128)(2,1)S(1)} %collective-permute-done.5), channel_id=1, source_target_pairs={{0,15},{1,0},{2,1},{3,2},{4,3},{5,4},{6,5},{7,6},{8,7},{9,8},{10,9... | collective-permute-start | bytes 331784 | tf_op jit(solution)/shard_map/ppermute | solution.py:29
  48.5 4.6 %collective-permute-start.9 = (bf16[72,768]{1,0:T(8,128)(2,1)S(1)}, bf16[72,768]{1,0:T(8,128)(2,1)}, u32[]{:S(2)}, u32[]{:S(2)}) collective-permute-start(bf16[72,768]{1,0:T(8,128)(2,1)S(1)} %collective-permute-done.7), channel_id=1, source_target_pairs={{0,15},{1,0},{2,1},{3,2},{4,3},{5,4},{6,5},{7,6},{8,7},{9,8},{10,9... | collective-permute-start | bytes 331784 | tf_op jit(solution)/shard_map/ppermute | solution.py:29
  57.3 4.7 %collective-permute-start.11 = (bf16[72,768]{1,0:T(8,128)(2,1)}, bf16[72,768]{1,0:T(8,128)(2,1)}, u32[]{:S(2)}, u32[]{:S(2)}) collective-permute-start(bf16[72,768]{1,0:T(8,128)(2,1)} %collective-permute-done.9), channel_id=1, source_target_pairs={{0,15},{1,0},{2,1},{3,2},{4,3},{5,4},{6,5},{7,6},{8,7},{9,8},{10,9... | collective-permute-start | bytes 331784 | tf_op jit(solution)/shard_map/ppermute | solution.py:29
  66.4 3.4 %dynamic_update_slice.96 = bf16[1152,768]{0,1:T(8,128)(2,1)} dynamic-update-slice(bf16[1152,768]{0,1:T(8,128)(2,1)} %broadcast.105.clone, bf16[72,768]{0,1:T(8,128)(2,1)S(1)} %copy.14, s32[]{:T(128)S(6)} %select_n.203, s32[]{:T(128)} %constant.159.clone.1) | dynamic-update-slice | bytes 221188 | tf_op jit(solution)/shard_map/dynamic_update_slice | solution.py:20
  69.7 4.2 %collective-permute-start.13 = (bf16[72,768]{1,0:T(8,128)(2,1)}, bf16[72,768]{1,0:T(8,128)(2,1)}, u32[]{:S(2)}, u32[]{:S(2)}) collective-permute-start(bf16[72,768]{1,0:T(8,128)(2,1)} %collective-permute-done.11), channel_id=1, source_target_pairs={{0,15},{1,0},{2,1},{3,2},{4,3},{5,4},{6,5},{7,6},{8,7},{9,8},{10,9... | collective-permute-start | bytes 331784 | tf_op jit(solution)/shard_map/ppermute | solution.py:29
  77.5 3.8 %dynamic_update_slice.98 = bf16[1152,768]{0,1:T(8,128)(2,1)} dynamic-update-slice(bf16[1152,768]{0,1:T(8,128)(2,1)} %dynamic_update_slice.97, bf16[72,768]{0,1:T(8,128)(2,1)S(1)} %copy.16, s32[]{:T(128)S(6)} %select_n.207, s32[]{:T(128)} %constant.159.clone.1) | dynamic-update-slice | bytes 221188 | tf_op jit(solution)/shard_map/dynamic_update_slice | solution.py:30
  81.5 3.8 %dynamic_update_slice.99 = bf16[1152,768]{0,1:T(8,128)(2,1)} dynamic-update-slice(bf16[1152,768]{0,1:T(8,128)(2,1)} %dynamic_update_slice.98, bf16[72,768]{0,1:T(8,128)(2,1)S(1)} %copy.17, s32[]{:T(128)S(6)} %select_n.209, s32[]{:T(128)} %constant.159.clone.1) | dynamic-update-slice | bytes 221188 | tf_op jit(solution)/shard_map/dynamic_update_slice | solution.py:25
  85.4 3.8 %dynamic_update_slice.100 = bf16[1152,768]{0,1:T(8,128)(2,1)} dynamic-update-slice(bf16[1152,768]{0,1:T(8,128)(2,1)} %dynamic_update_slice.99, bf16[72,768]{0,1:T(8,128)(2,1)S(1)} %copy.18, s32[]{:T(128)S(6)} %select_n.211, s32[]{:T(128)} %constant.159.clone.1) | dynamic-update-slice | bytes 221188 | tf_op jit(solution)/shard_map/dynamic_update_slice | solution.py:30
  89.4 3.8 %dynamic_update_slice.101 = bf16[1152,768]{0,1:T(8,128)(2,1)} dynamic-update-slice(bf16[1152,768]{0,1:T(8,128)(2,1)} %dynamic_update_slice.100, bf16[72,768]{0,1:T(8,128)(2,1)S(1)} %copy.19, s32[]{:T(128)S(6)} %select_n.213, s32[]{:T(128)} %constant.159.clone.1) | dynamic-update-slice | bytes 221188 | tf_op jit(solution)/shard_map/dynamic_update_slice | solution.py:25
  93.3 3.8 %dynamic_update_slice.102 = bf16[1152,768]{0,1:T(8,128)(2,1)} dynamic-update-slice(bf16[1152,768]{0,1:T(8,128)(2,1)} %dynamic_update_slice.101, bf16[72,768]{0,1:T(8,128)(2,1)S(1)} %copy.20, s32[]{:T(128)S(6)} %select_n.215, s32[]{:T(128)} %constant.159.clone.1) | dynamic-update-slice | bytes 221188 | tf_op jit(solution)/shard_map/dynamic_update_slice | solution.py:30
  97.2 3.7 %dynamic_update_slice.103 = bf16[1152,768]{0,1:T(8,128)(2,1)} dynamic-update-slice(bf16[1152,768]{0,1:T(8,128)(2,1)} %dynamic_update_slice.102, bf16[72,768]{0,1:T(8,128)(2,1)S(1)} %copy.21, s32[]{:T(128)S(6)} %select_n.217, s32[]{:T(128)} %constant.159.clone.1) | dynamic-update-slice | bytes 221188 | tf_op jit(solution)/shard_map/dynamic_update_slice | solution.py:25
  101.1 3.7 %dynamic_update_slice.104 = bf16[1152,768]{0,1:T(8,128)(2,1)} dynamic-update-slice(bf16[1152,768]{0,1:T(8,128)(2,1)} %dynamic_update_slice.103, bf16[72,768]{0,1:T(8,128)(2,1)S(1)} %copy.22, s32[]{:T(128)S(6)} %select_n.219, s32[]{:T(128)} %constant.159.clone.1) | dynamic-update-slice | bytes 221188 | tf_op jit(solution)/shard_map/dynamic_update_slice | solution.py:30
  105.0 3.7 %dynamic_update_slice.105 = bf16[1152,768]{0,1:T(8,128)(2,1)} dynamic-update-slice(bf16[1152,768]{0,1:T(8,128)(2,1)} %dynamic_update_slice.104, bf16[72,768]{0,1:T(8,128)(2,1)S(1)} %copy.23, s32[]{:T(128)S(6)} %select_n.221, s32[]{:T(128)} %constant.159.clone.1) | dynamic-update-slice | bytes 221188 | tf_op jit(solution)/shard_map/dynamic_update_slice | solution.py:25
  109.8 3.7 %dynamic_update_slice.106 = bf16[1152,768]{0,1:T(8,128)(2,1)} dynamic-update-slice(bf16[1152,768]{0,1:T(8,128)(2,1)} %dynamic_update_slice.105, bf16[72,768]{0,1:T(8,128)(2,1)S(1)} %copy.24, s32[]{:T(128)S(6)} %select_n.223, s32[]{:T(128)} %constant.159.clone.1) | dynamic-update-slice | bytes 221188 | tf_op jit(solution)/shard_map/dynamic_update_slice | solution.py:30
  114.6 3.7 %dynamic_update_slice.107 = bf16[1152,768]{0,1:T(8,128)(2,1)} dynamic-update-slice(bf16[1152,768]{0,1:T(8,128)(2,1)} %dynamic_update_slice.106, bf16[72,768]{0,1:T(8,128)(2,1)S(1)} %copy.25, s32[]{:T(128)S(6)} %select_n.225, s32[]{:T(128)} %constant.159.clone.1) | dynamic-update-slice | bytes 221188 | tf_op jit(solution)/shard_map/dynamic_update_slice | solution.py:25
  119.4 3.7 %dynamic_update_slice.108 = bf16[1152,768]{0,1:T(8,128)(2,1)} dynamic-update-slice(bf16[1152,768]{0,1:T(8,128)(2,1)} %dynamic_update_slice.107, bf16[72,768]{0,1:T(8,128)(2,1)S(1)} %copy.26, s32[]{:T(128)S(6)} %select_n.227, s32[]{:T(128)} %constant.159.clone.1) | dynamic-update-slice | bytes 221188 | tf_op jit(solution)/shard_map/dynamic_update_slice | solution.py:30
  124.2 3.7 %dynamic_update_slice.109 = bf16[1152,768]{0,1:T(8,128)(2,1)} dynamic-update-slice(bf16[1152,768]{0,1:T(8,128)(2,1)} %dynamic_update_slice.108, bf16[72,768]{0,1:T(8,128)(2,1)S(1)} %copy.27, s32[]{:T(128)S(6)} %select_n.229, s32[]{:T(128)} %constant.159.clone.1) | dynamic-update-slice | bytes 221188 | tf_op jit(solution)/shard_map/dynamic_update_slice | solution.py:25
  129.1 3.7 %dynamic_update_slice.110 = bf16[1152,768]{0,1:T(8,128)(2,1)} dynamic-update-slice(bf16[1152,768]{0,1:T(8,128)(2,1)} %dynamic_update_slice.109, bf16[72,768]{0,1:T(8,128)(2,1)S(1)} %copy.28, s32[]{:T(128)S(6)} %select_n.231, s32[]{:T(128)} %constant.159.clone.1) | dynamic-update-slice | bytes 221188 | tf_op jit(solution)/shard_map/dynamic_update_slice | solution.py:30
  133.9 3.7 %dynamic_update_slice.111 = bf16[1152,768]{0,1:T(8,128)(2,1)} dynamic-update-slice(bf16[1152,768]{0,1:T(8,128)(2,1)} %dynamic_update_slice.110, bf16[72,768]{0,1:T(8,128)(2,1)S(1)} %copy.29, s32[]{:T(128)S(6)} %select_n.233, s32[]{:T(128)} %constant.159.clone.1) | dynamic-update-slice | bytes 221188 | tf_op jit(solution)/shard_map/dynamic_update_slice | solution.py:25
  141.5 3.9 %copy.32 = bf16[1152,768]{0,1:T(8,128)(2,1)} copy(bf16[1152,768]{1,0:T(8,128)(2,1)} %all-gather.3.cloned.1.call-done) | data formatting | bytes 3538944 | tf_op jit(solution)/shard_map/all_gather | solution.py:76
  150.3 6.5 %collective-permute-done.15 = bf16[72,1536]{1,0:T(8,128)(2,1)S(1)} collective-permute-done((bf16[72,1536]{1,0:T(8,128)(2,1)S(1)}, bf16[72,1536]{1,0:T(8,128)(2,1)S(1)}, u32[]{:S(2)}, u32[]{:S(2)}) %collective-permute-start.15) | collective-permute-done | bytes 221216 | tf_op jit(solution)/shard_map/ppermute | solution.py:39
  162.4 4.4 %collective-permute-start.17 = (bf16[72,768]{1,0:T(8,128)(2,1)S(1)}, bf16[72,768]{1,0:T(8,128)(2,1)S(1)}, u32[]{:S(2)}, u32[]{:S(2)}) collective-permute-start(bf16[72,768]{1,0:T(8,128)(2,1)S(1)} %convolution_convert_fusion.1), channel_id=1, source_target_pairs={{0,15},{1,0},{2,1},{3,2},{4,3},{5,4},{6,5},{7,6},{8,7},{9,8},{10,9... | collective-permute-start | bytes 331784 | tf_op jit(solution)/shard_map/ppermute | solution.py:29
  169.4 4.5 %collective-permute-start.19 = (bf16[72,768]{1,0:T(8,128)(2,1)S(1)}, bf16[72,768]{1,0:T(8,128)(2,1)S(1)}, u32[]{:S(2)}, u32[]{:S(2)}) collective-permute-start(bf16[72,768]{1,0:T(8,128)(2,1)S(1)} %collective-permute-done.17), channel_id=1, source_target_pairs={{0,15},{1,0},{2,1},{3,2},{4,3},{5,4},{6,5},{7,6},{8,7},{9,8},{10,9... | collective-permute-start | bytes 331784 | tf_op jit(solution)/shard_map/ppermute | solution.py:29
  176.6 4.5 %collective-permute-start.21 = (bf16[72,768]{1,0:T(8,128)(2,1)S(1)}, bf16[72,768]{1,0:T(8,128)(2,1)S(1)}, u32[]{:S(2)}, u32[]{:S(2)}) collective-permute-start(bf16[72,768]{1,0:T(8,128)(2,1)S(1)} %collective-permute-done.19), channel_id=1, source_target_pairs={{0,15},{1,0},{2,1},{3,2},{4,3},{5,4},{6,5},{7,6},{8,7},{9,8},{10,9... | collective-permute-start | bytes 331784 | tf_op jit(solution)/shard_map/ppermute | solution.py:29
  183.6 4.5 %collective-permute-start.23 = (bf16[72,768]{1,0:T(8,128)(2,1)S(1)}, bf16[72,768]{1,0:T(8,128)(2,1)S(1)}, u32[]{:S(2)}, u32[]{:S(2)}) collective-permute-start(bf16[72,768]{1,0:T(8,128)(2,1)S(1)} %collective-permute-done.21), channel_id=1, source_target_pairs={{0,15},{1,0},{2,1},{3,2},{4,3},{5,4},{6,5},{7,6},{8,7},{9,8},{10,9... | collective-permute-start | bytes 331784 | tf_op jit(solution)/shard_map/ppermute | solution.py:29
  188.1 4.6 %collective-permute-done.22 = bf16[72,768]{1,0:T(8,128)(2,1)S(1)} collective-permute-done((bf16[72,768]{1,0:T(8,128)(2,1)S(1)}, bf16[72,768]{1,0:T(8,128)(2,1)S(1)}, u32[]{:S(2)}, u32[]{:S(2)}) %collective-permute-start.22) | collective-permute-done | bytes 110624 | tf_op jit(solution)/shard_map/ppermute | solution.py:24
  192.7 4.4 %collective-permute-start.25 = (bf16[72,768]{1,0:T(8,128)(2,1)S(1)}, bf16[72,768]{1,0:T(8,128)(2,1)S(1)}, u32[]{:S(2)}, u32[]{:S(2)}) collective-permute-start(bf16[72,768]{1,0:T(8,128)(2,1)S(1)} %collective-permute-done.23), channel_id=1, source_target_pairs={{0,15},{1,0},{2,1},{3,2},{4,3},{5,4},{6,5},{7,6},{8,7},{9,8},{10,9... | collective-permute-start | bytes 331784 | tf_op jit(solution)/shard_map/ppermute | solution.py:29
  200.1 4.4 %collective-permute-start.27 = (bf16[72,768]{1,0:T(8,128)(2,1)S(1)}, bf16[72,768]{1,0:T(8,128)(2,1)}, u32[]{:S(2)}, u32[]{:S(2)}) collective-permute-start(bf16[72,768]{1,0:T(8,128)(2,1)S(1)} %collective-permute-done.25), channel_id=1, source_target_pairs={{0,15},{1,0},{2,1},{3,2},{4,3},{5,4},{6,5},{7,6},{8,7},{9,8},{10,9... | collective-permute-start | bytes 331784 | tf_op jit(solution)/shard_map/ppermute | solution.py:29
  207.1 4.5 %collective-permute-start.29 = (bf16[72,768]{1,0:T(8,128)(2,1)}, bf16[72,768]{1,0:T(8,128)(2,1)}, u32[]{:S(2)}, u32[]{:S(2)}) collective-permute-start(bf16[72,768]{1,0:T(8,128)(2,1)} %collective-permute-done.27), channel_id=1, source_target_pairs={{0,15},{1,0},{2,1},{3,2},{4,3},{5,4},{6,5},{7,6},{8,7},{9,8},{10,9... | collective-permute-start | bytes 331784 | tf_op jit(solution)/shard_map/ppermute | solution.py:29
  224.8 3.8 %dynamic_update_slice.114 = bf16[1152,768]{0,1:T(8,128)(2,1)} dynamic-update-slice(bf16[1152,768]{0,1:T(8,128)(2,1)} %dynamic_update_slice.113, bf16[72,768]{0,1:T(8,128)(2,1)S(1)} %copy.37, s32[]{:T(128)S(6)} %select_n.207, s32[]{:T(128)} %constant.159.clone.1) | dynamic-update-slice | bytes 221188 | tf_op jit(solution)/shard_map/dynamic_update_slice | solution.py:30
  229.7 3.8 %dynamic_update_slice.115 = bf16[1152,768]{0,1:T(8,128)(2,1)} dynamic-update-slice(bf16[1152,768]{0,1:T(8,128)(2,1)} %dynamic_update_slice.114, bf16[72,768]{0,1:T(8,128)(2,1)S(1)} %copy.38, s32[]{:T(128)S(6)} %select_n.209, s32[]{:T(128)} %constant.159.clone.1) | dynamic-update-slice | bytes 221188 | tf_op jit(solution)/shard_map/dynamic_update_slice | solution.py:25
  234.5 3.8 %dynamic_update_slice.116 = bf16[1152,768]{0,1:T(8,128)(2,1)} dynamic-update-slice(bf16[1152,768]{0,1:T(8,128)(2,1)} %dynamic_update_slice.115, bf16[72,768]{0,1:T(8,128)(2,1)S(1)} %copy.39, s32[]{:T(128)S(6)} %select_n.211, s32[]{:T(128)} %constant.159.clone.1) | dynamic-update-slice | bytes 221188 | tf_op jit(solution)/shard_map/dynamic_update_slice | solution.py:30
  239.3 3.8 %dynamic_update_slice.117 = bf16[1152,768]{0,1:T(8,128)(2,1)} dynamic-update-slice(bf16[1152,768]{0,1:T(8,128)(2,1)} %dynamic_update_slice.116, bf16[72,768]{0,1:T(8,128)(2,1)S(1)} %copy.40, s32[]{:T(128)S(6)} %select_n.213, s32[]{:T(128)} %constant.159.clone.1) | dynamic-update-slice | bytes 221188 | tf_op jit(solution)/shard_map/dynamic_update_slice | solution.py:25
  243.2 3.8 %dynamic_update_slice.118 = bf16[1152,768]{0,1:T(8,128)(2,1)} dynamic-update-slice(bf16[1152,768]{0,1:T(8,128)(2,1)} %dynamic_update_slice.117, bf16[72,768]{0,1:T(8,128)(2,1)S(1)} %copy.41, s32[]{:T(128)S(6)} %select_n.215, s32[]{:T(128)} %constant.159.clone.1) | dynamic-update-slice | bytes 221188 | tf_op jit(solution)/shard_map/dynamic_update_slice | solution.py:30
  248.1 3.7 %dynamic_update_slice.119 = bf16[1152,768]{0,1:T(8,128)(2,1)} dynamic-update-slice(bf16[1152,768]{0,1:T(8,128)(2,1)} %dynamic_update_slice.118, bf16[72,768]{0,1:T(8,128)(2,1)S(1)} %copy.42, s32[]{:T(128)S(6)} %select_n.217, s32[]{:T(128)} %constant.159.clone.1) | dynamic-update-slice | bytes 221188 | tf_op jit(solution)/shard_map/dynamic_update_slice | solution.py:25
  252.9 3.7 %dynamic_update_slice.120 = bf16[1152,768]{0,1:T(8,128)(2,1)} dynamic-update-slice(bf16[1152,768]{0,1:T(8,128)(2,1)} %dynamic_update_slice.119, bf16[72,768]{0,1:T(8,128)(2,1)S(1)} %copy.43, s32[]{:T(128)S(6)} %select_n.219, s32[]{:T(128)} %constant.159.clone.1) | dynamic-update-slice | bytes 221188 | tf_op jit(solution)/shard_map/dynamic_update_slice | solution.py:30
  257.7 3.7 %dynamic_update_slice.121 = bf16[1152,768]{0,1:T(8,128)(2,1)} dynamic-update-slice(bf16[1152,768]{0,1:T(8,128)(2,1)} %dynamic_update_slice.120, bf16[72,768]{0,1:T(8,128)(2,1)S(1)} %copy.44, s32[]{:T(128)S(6)} %select_n.221, s32[]{:T(128)} %constant.159.clone.1) | dynamic-update-slice | bytes 221188 | tf_op jit(solution)/shard_map/dynamic_update_slice | solution.py:25
  261.6 3.7 %dynamic_update_slice.122 = bf16[1152,768]{0,1:T(8,128)(2,1)} dynamic-update-slice(bf16[1152,768]{0,1:T(8,128)(2,1)} %dynamic_update_slice.121, bf16[72,768]{0,1:T(8,128)(2,1)S(1)} %copy.45, s32[]{:T(128)S(6)} %select_n.223, s32[]{:T(128)} %constant.159.clone.1) | dynamic-update-slice | bytes 221188 | tf_op jit(solution)/shard_map/dynamic_update_slice | solution.py:30
  266.4 3.7 %dynamic_update_slice.123 = bf16[1152,768]{0,1:T(8,128)(2,1)} dynamic-update-slice(bf16[1152,768]{0,1:T(8,128)(2,1)} %dynamic_update_slice.122, bf16[72,768]{0,1:T(8,128)(2,1)S(1)} %copy.46, s32[]{:T(128)S(6)} %select_n.225, s32[]{:T(128)} %constant.159.clone.1) | dynamic-update-slice | bytes 221188 | tf_op jit(solution)/shard_map/dynamic_update_slice | solution.py:25
  271.2 3.7 %dynamic_update_slice.124 = bf16[1152,768]{0,1:T(8,128)(2,1)} dynamic-update-slice(bf16[1152,768]{0,1:T(8,128)(2,1)} %dynamic_update_slice.123, bf16[72,768]{0,1:T(8,128)(2,1)S(1)} %copy.47, s32[]{:T(128)S(6)} %select_n.227, s32[]{:T(128)} %constant.159.clone.1) | dynamic-update-slice | bytes 221188 | tf_op jit(solution)/shard_map/dynamic_update_slice | solution.py:30
  275.1 3.7 %dynamic_update_slice.125 = bf16[1152,768]{0,1:T(8,128)(2,1)} dynamic-update-slice(bf16[1152,768]{0,1:T(8,128)(2,1)} %dynamic_update_slice.124, bf16[72,768]{0,1:T(8,128)(2,1)S(1)} %copy.48, s32[]{:T(128)S(6)} %select_n.229, s32[]{:T(128)} %constant.159.clone.1) | dynamic-update-slice | bytes 221188 | tf_op jit(solution)/shard_map/dynamic_update_slice | solution.py:25
  279.9 3.7 %dynamic_update_slice.126 = bf16[1152,768]{0,1:T(8,128)(2,1)} dynamic-update-slice(bf16[1152,768]{0,1:T(8,128)(2,1)} %dynamic_update_slice.125, bf16[72,768]{0,1:T(8,128)(2,1)S(1)} %copy.49, s32[]{:T(128)S(6)} %select_n.231, s32[]{:T(128)} %constant.159.clone.1) | dynamic-update-slice | bytes 221188 | tf_op jit(solution)/shard_map/dynamic_update_slice | solution.py:30
  284.7 3.7 %dynamic_update_slice.127 = bf16[1152,768]{0,1:T(8,128)(2,1)} dynamic-update-slice(bf16[1152,768]{0,1:T(8,128)(2,1)} %dynamic_update_slice.126, bf16[72,768]{0,1:T(8,128)(2,1)S(1)} %copy.50, s32[]{:T(128)S(6)} %select_n.233, s32[]{:T(128)} %constant.159.clone.1) | dynamic-update-slice | bytes 221188 | tf_op jit(solution)/shard_map/dynamic_update_slice | solution.py:25
  292.4 3.9 %copy.53 = bf16[1152,768]{0,1:T(8,128)(2,1)} copy(bf16[1152,768]{1,0:T(8,128)(2,1)} %all-gather.5.cloned.1.call-done) | data formatting | bytes 3538944 | tf_op jit(solution)/shard_map/all_gather | solution.py:76
  (180 shorter events, 97.1 us)
Async XLA Ops:
  7.2 141.2 %copy-start = (bf16[768,1536]{1,0:T(8,128)(2,1)S(1)}, bf16[768,1536]{1,0:T(8,128)(2,1)}, u32[]{:S(2)}) copy-start(bf16[768,1536]{1,0:T(8,128)(2,1)} %param.15) | copy-start | bytes 7077892
  7.2 134.3 %all-gather.3.cloned.1.call-start = ((), (), s32[]{:S(2)}) async-start(), calls=%async_computation | async-start | bytes 1880064 | tf_op jit(solution)/shard_map/all_gather | solution.py:76
  15.7 276.7 %all-gather.5.cloned.1.call-start = ((), (), s32[]{:S(2)}) async-start(), calls=%async_computation.1 | async-start | bytes 1880064 | tf_op jit(solution)/shard_map/all_gather | solution.py:76
  15.7 46.9 %copy-start.1 = (bf16[1536,768]{1,0:T(8,128)(2,1)S(1)}, bf16[1536,768]{1,0:T(8,128)(2,1)}, u32[]{:S(2)}) copy-start(bf16[1536,768]{1,0:T(8,128)(2,1)} %param.12) | copy-start | bytes 7077892
  18.1 8.1 %collective-permute-start = (bf16[72,768]{1,0:T(8,128)(2,1)S(1)}, bf16[72,768]{1,0:T(8,128)(2,1)S(1)}, u32[]{:S(2)}, u32[]{:S(2)}) collective-permute-start(bf16[72,768]{1,0:T(8,128)(2,1)S(1)} %convolution_convert_fusion.4), channel_id=1, source_target_pairs={{0,1},{1,2},{2,3},{3,4},{4,5},{5,6},{6,7},{7,8},{8,9},{9,10},{10,1... | collective-permute-start | bytes 331784 | tf_op jit(solution)/shard_map/ppermute | solution.py:24
  18.7 7.5 %collective-permute-start.1 = (bf16[72,768]{1,0:T(8,128)(2,1)S(1)}, bf16[72,768]{1,0:T(8,128)(2,1)S(1)}, u32[]{:S(2)}, u32[]{:S(2)}) collective-permute-start(bf16[72,768]{1,0:T(8,128)(2,1)S(1)} %convolution_convert_fusion.4), channel_id=1, source_target_pairs={{0,15},{1,0},{2,1},{3,2},{4,3},{5,4},{6,5},{7,6},{8,7},{9,8},{10,9... | collective-permute-start | bytes 331784 | tf_op jit(solution)/shard_map/ppermute | solution.py:29
  26.2 8.3 %collective-permute-start.2 = (bf16[72,768]{1,0:T(8,128)(2,1)S(1)}, bf16[72,768]{1,0:T(8,128)(2,1)S(1)}, u32[]{:S(2)}, u32[]{:S(2)}) collective-permute-start(bf16[72,768]{1,0:T(8,128)(2,1)S(1)} %collective-permute-done), channel_id=1, source_target_pairs={{0,1},{1,2},{2,3},{3,4},{4,5},{5,6},{6,7},{7,8},{8,9},{9,10},{10,1... | collective-permute-start | bytes 331784 | tf_op jit(solution)/shard_map/ppermute | solution.py:24
  26.2 8.3 %collective-permute-start.3 = (bf16[72,768]{1,0:T(8,128)(2,1)S(1)}, bf16[72,768]{1,0:T(8,128)(2,1)S(1)}, u32[]{:S(2)}, u32[]{:S(2)}) collective-permute-start(bf16[72,768]{1,0:T(8,128)(2,1)S(1)} %collective-permute-done.1), channel_id=1, source_target_pairs={{0,15},{1,0},{2,1},{3,2},{4,3},{5,4},{6,5},{7,6},{8,7},{9,8},{10,9... | collective-permute-start | bytes 331784 | tf_op jit(solution)/shard_map/ppermute | solution.py:29
  34.5 7.0 %collective-permute-start.4 = (bf16[72,768]{1,0:T(8,128)(2,1)S(1)}, bf16[72,768]{1,0:T(8,128)(2,1)S(1)}, u32[]{:S(2)}, u32[]{:S(2)}) collective-permute-start(bf16[72,768]{1,0:T(8,128)(2,1)S(1)} %collective-permute-done.2), channel_id=1, source_target_pairs={{0,1},{1,2},{2,3},{3,4},{4,5},{5,6},{6,7},{7,8},{8,9},{9,10},{10,1... | collective-permute-start | bytes 331784 | tf_op jit(solution)/shard_map/ppermute | solution.py:24
  34.5 7.0 %collective-permute-start.5 = (bf16[72,768]{1,0:T(8,128)(2,1)S(1)}, bf16[72,768]{1,0:T(8,128)(2,1)S(1)}, u32[]{:S(2)}, u32[]{:S(2)}) collective-permute-start(bf16[72,768]{1,0:T(8,128)(2,1)S(1)} %collective-permute-done.3), channel_id=1, source_target_pairs={{0,15},{1,0},{2,1},{3,2},{4,3},{5,4},{6,5},{7,6},{8,7},{9,8},{10,9... | collective-permute-start | bytes 331784 | tf_op jit(solution)/shard_map/ppermute | solution.py:29
  41.5 21.2 %copy-start.7 = (bf16[72,768]{1,0:T(8,128)(2,1)}, bf16[72,768]{1,0:T(8,128)(2,1)S(1)}, u32[]{:S(2)}) copy-start(bf16[72,768]{1,0:T(8,128)(2,1)S(1)} %collective-permute-done.4) | copy-start | bytes 331780
  41.5 7.0 %collective-permute-start.6 = (bf16[72,768]{1,0:T(8,128)(2,1)S(1)}, bf16[72,768]{1,0:T(8,128)(2,1)S(1)}, u32[]{:S(2)}, u32[]{:S(2)}) collective-permute-start(bf16[72,768]{1,0:T(8,128)(2,1)S(1)} %collective-permute-done.4), channel_id=1, source_target_pairs={{0,1},{1,2},{2,3},{3,4},{4,5},{5,6},{6,7},{7,8},{8,9},{9,10},{10,1... | collective-permute-start | bytes 331784 | tf_op jit(solution)/shard_map/ppermute | solution.py:24
  41.5 21.1 %copy-start.9 = (bf16[72,768]{1,0:T(8,128)(2,1)}, bf16[72,768]{1,0:T(8,128)(2,1)S(1)}, u32[]{:S(2)}) copy-start(bf16[72,768]{1,0:T(8,128)(2,1)S(1)} %collective-permute-done.5) | copy-start | bytes 331780
  41.5 7.0 %collective-permute-start.7 = (bf16[72,768]{1,0:T(8,128)(2,1)S(1)}, bf16[72,768]{1,0:T(8,128)(2,1)S(1)}, u32[]{:S(2)}, u32[]{:S(2)}) collective-permute-start(bf16[72,768]{1,0:T(8,128)(2,1)S(1)} %collective-permute-done.5), channel_id=1, source_target_pairs={{0,15},{1,0},{2,1},{3,2},{4,3},{5,4},{6,5},{7,6},{8,7},{9,8},{10,9... | collective-permute-start | bytes 331784 | tf_op jit(solution)/shard_map/ppermute | solution.py:29
  48.4 7.0 %collective-permute-start.8 = (bf16[72,768]{1,0:T(8,128)(2,1)S(1)}, bf16[72,768]{1,0:T(8,128)(2,1)S(1)}, u32[]{:S(2)}, u32[]{:S(2)}) collective-permute-start(bf16[72,768]{1,0:T(8,128)(2,1)S(1)} %collective-permute-done.6), channel_id=1, source_target_pairs={{0,1},{1,2},{2,3},{3,4},{4,5},{5,6},{6,7},{7,8},{8,9},{9,10},{10,1... | collective-permute-start | bytes 331784 | tf_op jit(solution)/shard_map/ppermute | solution.py:24
  48.5 8.8 %collective-permute-start.9 = (bf16[72,768]{1,0:T(8,128)(2,1)S(1)}, bf16[72,768]{1,0:T(8,128)(2,1)}, u32[]{:S(2)}, u32[]{:S(2)}) collective-permute-start(bf16[72,768]{1,0:T(8,128)(2,1)S(1)} %collective-permute-done.7), channel_id=1, source_target_pairs={{0,15},{1,0},{2,1},{3,2},{4,3},{5,4},{6,5},{7,6},{8,7},{9,8},{10,9... | collective-permute-start | bytes 331784 | tf_op jit(solution)/shard_map/ppermute | solution.py:29
  55.4 7.1 %collective-permute-start.10 = (bf16[72,768]{1,0:T(8,128)(2,1)S(1)}, bf16[72,768]{1,0:T(8,128)(2,1)}, u32[]{:S(2)}, u32[]{:S(2)}) collective-permute-start(bf16[72,768]{1,0:T(8,128)(2,1)S(1)} %collective-permute-done.8), channel_id=1, source_target_pairs={{0,1},{1,2},{2,3},{3,4},{4,5},{5,6},{6,7},{7,8},{8,9},{9,10},{10,1... | collective-permute-start | bytes 331784 | tf_op jit(solution)/shard_map/ppermute | solution.py:24
  57.3 12.5 %collective-permute-start.11 = (bf16[72,768]{1,0:T(8,128)(2,1)}, bf16[72,768]{1,0:T(8,128)(2,1)}, u32[]{:S(2)}, u32[]{:S(2)}) collective-permute-start(bf16[72,768]{1,0:T(8,128)(2,1)} %collective-permute-done.9), channel_id=1, source_target_pairs={{0,15},{1,0},{2,1},{3,2},{4,3},{5,4},{6,5},{7,6},{8,7},{9,8},{10,9... | collective-permute-start | bytes 331784 | tf_op jit(solution)/shard_map/ppermute | solution.py:29
  62.5 11.4 %collective-permute-start.12 = (bf16[72,768]{1,0:T(8,128)(2,1)}, bf16[72,768]{1,0:T(8,128)(2,1)}, u32[]{:S(2)}, u32[]{:S(2)}) collective-permute-start(bf16[72,768]{1,0:T(8,128)(2,1)} %collective-permute-done.10), channel_id=1, source_target_pairs={{0,1},{1,2},{2,3},{3,4},{4,5},{5,6},{6,7},{7,8},{8,9},{9,10},{10,1... | collective-permute-start | bytes 331784 | tf_op jit(solution)/shard_map/ppermute | solution.py:24
  66.4 22.9 %copy-start.8 = (bf16[72,768]{1,0:T(8,128)(2,1)S(1)}, bf16[72,768]{1,0:T(8,128)(2,1)}, u32[]{:S(2)}) copy-start(bf16[72,768]{1,0:T(8,128)(2,1)} %copy-done.7) | copy-start | bytes 331780
  69.7 58.3 %collective-permute-start.13 = (bf16[72,768]{1,0:T(8,128)(2,1)}, bf16[72,768]{1,0:T(8,128)(2,1)}, u32[]{:S(2)}, u32[]{:S(2)}) collective-permute-start(bf16[72,768]{1,0:T(8,128)(2,1)} %collective-permute-done.11), channel_id=1, source_target_pairs={{0,15},{1,0},{2,1},{3,2},{4,3},{5,4},{6,5},{7,6},{8,7},{9,8},{10,9... | collective-permute-start | bytes 331784 | tf_op jit(solution)/shard_map/ppermute | solution.py:29
  73.9 58.9 %collective-permute-start.14 = (bf16[72,768]{1,0:T(8,128)(2,1)}, bf16[72,768]{1,0:T(8,128)(2,1)}, u32[]{:S(2)}, u32[]{:S(2)}) collective-permute-start(bf16[72,768]{1,0:T(8,128)(2,1)} %collective-permute-done.12), channel_id=1, source_target_pairs={{0,1},{1,2},{2,3},{3,4},{4,5},{5,6},{6,7},{7,8},{8,9},{9,10},{10,1... | collective-permute-start | bytes 331784 | tf_op jit(solution)/shard_map/ppermute | solution.py:24
  77.5 19.6 %copy-start.12 = (bf16[72,768]{1,0:T(8,128)(2,1)S(1)}, bf16[72,768]{1,0:T(8,128)(2,1)}, u32[]{:S(2)}) copy-start(bf16[72,768]{1,0:T(8,128)(2,1)} %copy-done.11) | copy-start | bytes 331780
  149.0 7.8 %collective-permute-start.15 = (bf16[72,1536]{1,0:T(8,128)(2,1)S(1)}, bf16[72,1536]{1,0:T(8,128)(2,1)S(1)}, u32[]{:S(2)}, u32[]{:S(2)}) collective-permute-start(bf16[72,1536]{1,0:T(8,128)(2,1)S(1)} %get-tuple-element.7), channel_id=1, source_target_pairs={{4,0},{5,1},{6,2},{7,3},{8,4},{9,5},{10,6},{11,7},{12,8},{13,9},{1... | collective-permute-start | bytes 663560 | tf_op jit(solution)/shard_map/ppermute | solution.py:39
  159.9 54.4 %copy-start.2 = (bf16[1536,768]{1,0:T(8,128)(2,1)S(1)}, bf16[1536,768]{1,0:T(8,128)(2,1)}, u32[]{:S(2)}) copy-start(bf16[1536,768]{1,0:T(8,128)(2,1)} %param.12) | copy-start | bytes 7077892
  162.3 7.0 %collective-permute-start.16 = (bf16[72,768]{1,0:T(8,128)(2,1)S(1)}, bf16[72,768]{1,0:T(8,128)(2,1)S(1)}, u32[]{:S(2)}, u32[]{:S(2)}) collective-permute-start(bf16[72,768]{1,0:T(8,128)(2,1)S(1)} %convolution_convert_fusion.1), channel_id=1, source_target_pairs={{0,1},{1,2},{2,3},{3,4},{4,5},{5,6},{6,7},{7,8},{8,9},{9,10},{10,1... | collective-permute-start | bytes 331784 | tf_op jit(solution)/shard_map/ppermute | solution.py:24
  162.4 7.0 %collective-permute-start.17 = (bf16[72,768]{1,0:T(8,128)(2,1)S(1)}, bf16[72,768]{1,0:T(8,128)(2,1)S(1)}, u32[]{:S(2)}, u32[]{:S(2)}) collective-permute-start(bf16[72,768]{1,0:T(8,128)(2,1)S(1)} %convolution_convert_fusion.1), channel_id=1, source_target_pairs={{0,15},{1,0},{2,1},{3,2},{4,3},{5,4},{6,5},{7,6},{8,7},{9,8},{10,9... | collective-permute-start | bytes 331784 | tf_op jit(solution)/shard_map/ppermute | solution.py:29
  169.3 44.6 %copy-start.20 = (bf16[72,768]{1,0:T(8,128)(2,1)}, bf16[72,768]{1,0:T(8,128)(2,1)S(1)}, u32[]{:S(2)}) copy-start(bf16[72,768]{1,0:T(8,128)(2,1)S(1)} %collective-permute-done.16) | copy-start | bytes 331780
  169.3 7.3 %collective-permute-start.18 = (bf16[72,768]{1,0:T(8,128)(2,1)S(1)}, bf16[72,768]{1,0:T(8,128)(2,1)S(1)}, u32[]{:S(2)}, u32[]{:S(2)}) collective-permute-start(bf16[72,768]{1,0:T(8,128)(2,1)S(1)} %collective-permute-done.16), channel_id=1, source_target_pairs={{0,1},{1,2},{2,3},{3,4},{4,5},{5,6},{6,7},{7,8},{8,9},{9,10},{10,1... | collective-permute-start | bytes 331784 | tf_op jit(solution)/shard_map/ppermute | solution.py:24
  169.4 45.0 %copy-start.17 = (bf16[72,768]{1,0:T(8,128)(2,1)}, bf16[72,768]{1,0:T(8,128)(2,1)S(1)}, u32[]{:S(2)}) copy-start(bf16[72,768]{1,0:T(8,128)(2,1)S(1)} %collective-permute-done.17) | copy-start | bytes 331780
  169.4 7.3 %collective-permute-start.19 = (bf16[72,768]{1,0:T(8,128)(2,1)S(1)}, bf16[72,768]{1,0:T(8,128)(2,1)S(1)}, u32[]{:S(2)}, u32[]{:S(2)}) collective-permute-start(bf16[72,768]{1,0:T(8,128)(2,1)S(1)} %collective-permute-done.17), channel_id=1, source_target_pairs={{0,15},{1,0},{2,1},{3,2},{4,3},{5,4},{6,5},{7,6},{8,7},{9,8},{10,9... | collective-permute-start | bytes 331784 | tf_op jit(solution)/shard_map/ppermute | solution.py:29
  176.6 37.4 %copy-start.19 = (bf16[72,768]{1,0:T(8,128)(2,1)}, bf16[72,768]{1,0:T(8,128)(2,1)S(1)}, u32[]{:S(2)}) copy-start(bf16[72,768]{1,0:T(8,128)(2,1)S(1)} %collective-permute-done.18) | copy-start | bytes 331780
  176.6 7.0 %collective-permute-start.20 = (bf16[72,768]{1,0:T(8,128)(2,1)S(1)}, bf16[72,768]{1,0:T(8,128)(2,1)S(1)}, u32[]{:S(2)}, u32[]{:S(2)}) collective-permute-start(bf16[72,768]{1,0:T(8,128)(2,1)S(1)} %collective-permute-done.18), channel_id=1, source_target_pairs={{0,1},{1,2},{2,3},{3,4},{4,5},{5,6},{6,7},{7,8},{8,9},{9,10},{10,1... | collective-permute-start | bytes 331784 | tf_op jit(solution)/shard_map/ppermute | solution.py:24
  176.6 37.3 %copy-start.21 = (bf16[72,768]{1,0:T(8,128)(2,1)}, bf16[72,768]{1,0:T(8,128)(2,1)S(1)}, u32[]{:S(2)}) copy-start(bf16[72,768]{1,0:T(8,128)(2,1)S(1)} %collective-permute-done.19) | copy-start | bytes 331780
  176.6 7.0 %collective-permute-start.21 = (bf16[72,768]{1,0:T(8,128)(2,1)S(1)}, bf16[72,768]{1,0:T(8,128)(2,1)S(1)}, u32[]{:S(2)}, u32[]{:S(2)}) collective-permute-start(bf16[72,768]{1,0:T(8,128)(2,1)S(1)} %collective-permute-done.19), channel_id=1, source_target_pairs={{0,15},{1,0},{2,1},{3,2},{4,3},{5,4},{6,5},{7,6},{8,7},{9,8},{10,9... | collective-permute-start | bytes 331784 | tf_op jit(solution)/shard_map/ppermute | solution.py:29
  183.6 30.4 %copy-start.22 = (bf16[72,768]{1,0:T(8,128)(2,1)}, bf16[72,768]{1,0:T(8,128)(2,1)S(1)}, u32[]{:S(2)}) copy-start(bf16[72,768]{1,0:T(8,128)(2,1)S(1)} %collective-permute-done.20) | copy-start | bytes 331780
  183.6 9.1 %collective-permute-start.22 = (bf16[72,768]{1,0:T(8,128)(2,1)S(1)}, bf16[72,768]{1,0:T(8,128)(2,1)S(1)}, u32[]{:S(2)}, u32[]{:S(2)}) collective-permute-start(bf16[72,768]{1,0:T(8,128)(2,1)S(1)} %collective-permute-done.20), channel_id=1, source_target_pairs={{0,1},{1,2},{2,3},{3,4},{4,5},{5,6},{6,7},{7,8},{8,9},{9,10},{10,1... | collective-permute-start | bytes 331784 | tf_op jit(solution)/shard_map/ppermute | solution.py:24
  183.6 30.4 %copy-start.23 = (bf16[72,768]{1,0:T(8,128)(2,1)}, bf16[72,768]{1,0:T(8,128)(2,1)S(1)}, u32[]{:S(2)}) copy-start(bf16[72,768]{1,0:T(8,128)(2,1)S(1)} %collective-permute-done.21) | copy-start | bytes 331780
  183.6 9.1 %collective-permute-start.23 = (bf16[72,768]{1,0:T(8,128)(2,1)S(1)}, bf16[72,768]{1,0:T(8,128)(2,1)S(1)}, u32[]{:S(2)}, u32[]{:S(2)}) collective-permute-start(bf16[72,768]{1,0:T(8,128)(2,1)S(1)} %collective-permute-done.21), channel_id=1, source_target_pairs={{0,15},{1,0},{2,1},{3,2},{4,3},{5,4},{6,5},{7,6},{8,7},{9,8},{10,9... | collective-permute-start | bytes 331784 | tf_op jit(solution)/shard_map/ppermute | solution.py:29
  192.7 21.3 %copy-start.25 = (bf16[72,768]{1,0:T(8,128)(2,1)}, bf16[72,768]{1,0:T(8,128)(2,1)S(1)}, u32[]{:S(2)}) copy-start(bf16[72,768]{1,0:T(8,128)(2,1)S(1)} %collective-permute-done.22) | copy-start | bytes 331780
  192.7 7.4 %collective-permute-start.24 = (bf16[72,768]{1,0:T(8,128)(2,1)S(1)}, bf16[72,768]{1,0:T(8,128)(2,1)S(1)}, u32[]{:S(2)}, u32[]{:S(2)}) collective-permute-start(bf16[72,768]{1,0:T(8,128)(2,1)S(1)} %collective-permute-done.22), channel_id=1, source_target_pairs={{0,1},{1,2},{2,3},{3,4},{4,5},{5,6},{6,7},{7,8},{8,9},{9,10},{10,1... | collective-permute-start | bytes 331784 | tf_op jit(solution)/shard_map/ppermute | solution.py:24
  192.7 21.3 %copy-start.26 = (bf16[72,768]{1,0:T(8,128)(2,1)}, bf16[72,768]{1,0:T(8,128)(2,1)S(1)}, u32[]{:S(2)}) copy-start(bf16[72,768]{1,0:T(8,128)(2,1)S(1)} %collective-permute-done.23) | copy-start | bytes 331780
  192.7 7.4 %collective-permute-start.25 = (bf16[72,768]{1,0:T(8,128)(2,1)S(1)}, bf16[72,768]{1,0:T(8,128)(2,1)S(1)}, u32[]{:S(2)}, u32[]{:S(2)}) collective-permute-start(bf16[72,768]{1,0:T(8,128)(2,1)S(1)} %collective-permute-done.23), channel_id=1, source_target_pairs={{0,15},{1,0},{2,1},{3,2},{4,3},{5,4},{6,5},{7,6},{8,7},{9,8},{10,9... | collective-permute-start | bytes 331784 | tf_op jit(solution)/shard_map/ppermute | solution.py:29
  200.1 7.0 %collective-permute-start.26 = (bf16[72,768]{1,0:T(8,128)(2,1)S(1)}, bf16[72,768]{1,0:T(8,128)(2,1)S(1)}, u32[]{:S(2)}, u32[]{:S(2)}) collective-permute-start(bf16[72,768]{1,0:T(8,128)(2,1)S(1)} %collective-permute-done.24), channel_id=1, source_target_pairs={{0,1},{1,2},{2,3},{3,4},{4,5},{5,6},{6,7},{7,8},{8,9},{9,10},{10,1... | collective-permute-start | bytes 331784 | tf_op jit(solution)/shard_map/ppermute | solution.py:24
  200.1 7.0 %collective-permute-start.27 = (bf16[72,768]{1,0:T(8,128)(2,1)S(1)}, bf16[72,768]{1,0:T(8,128)(2,1)}, u32[]{:S(2)}, u32[]{:S(2)}) collective-permute-start(bf16[72,768]{1,0:T(8,128)(2,1)S(1)} %collective-permute-done.25), channel_id=1, source_target_pairs={{0,15},{1,0},{2,1},{3,2},{4,3},{5,4},{6,5},{7,6},{8,7},{9,8},{10,9... | collective-permute-start | bytes 331784 | tf_op jit(solution)/shard_map/ppermute | solution.py:29
  207.1 6.9 %collective-permute-start.28 = (bf16[72,768]{1,0:T(8,128)(2,1)S(1)}, bf16[72,768]{1,0:T(8,128)(2,1)S(1)}, u32[]{:S(2)}, u32[]{:S(2)}) collective-permute-start(bf16[72,768]{1,0:T(8,128)(2,1)S(1)} %collective-permute-done.26), channel_id=1, source_target_pairs={{0,1},{1,2},{2,3},{3,4},{4,5},{5,6},{6,7},{7,8},{8,9},{9,10},{10,1... | collective-permute-start | bytes 331784 | tf_op jit(solution)/shard_map/ppermute | solution.py:24
  207.1 71.7 %collective-permute-start.29 = (bf16[72,768]{1,0:T(8,128)(2,1)}, bf16[72,768]{1,0:T(8,128)(2,1)}, u32[]{:S(2)}, u32[]{:S(2)}) collective-permute-start(bf16[72,768]{1,0:T(8,128)(2,1)} %collective-permute-done.27), channel_id=1, source_target_pairs={{0,15},{1,0},{2,1},{3,2},{4,3},{5,4},{6,5},{7,6},{8,7},{9,8},{10,9... | collective-permute-start | bytes 331784 | tf_op jit(solution)/shard_map/ppermute | solution.py:29
  214.0 69.6 %collective-permute-start.30 = (bf16[72,768]{1,0:T(8,128)(2,1)S(1)}, bf16[72,768]{1,0:T(8,128)(2,1)}, u32[]{:S(2)}, u32[]{:S(2)}) collective-permute-start(bf16[72,768]{1,0:T(8,128)(2,1)S(1)} %collective-permute-done.28), channel_id=1, source_target_pairs={{0,1},{1,2},{2,3},{3,4},{4,5},{5,6},{6,7},{7,8},{8,9},{9,10},{10,1... | collective-permute-start | bytes 331784 | tf_op jit(solution)/shard_map/ppermute | solution.py:24
  (17 other events, 195.3 us)
Sparse Core Ops, SparseCore 0:
  15.8 46.4 all-gather.2
  160.0 41.0 all-gather.4
